TPU v7x, 32 devices: a whole 2x2x4 slice. The times are simulated.
32 devices in a mesh: grp: 2 (over y), gz: 4 (over z), gy: 2 (over x), sa: 2 (over core).
Axes of the slice: x: 2, y: 2, z: 4, core: 2. Of those that a mesh axis runs over, the one named last changes fastest.
Arguments:
- field: float32 [8, 32, 16, 128], P('sa', ('grp', 'gz'), 'gy'), parts along dimension 1, may hold values from 0 to 2
- diffusion: float32 [8], P('sa'), may hold values from 0.02 to 0.16
- secrete: float32 [8, 65536], P('sa', ('grp', 'gz', 'gy')), parts along dimension 1, may hold values from 0 to 1
- uptake: float32 [8, 65536], P('sa', ('grp', 'gz', 'gy')), parts along dimension 1, may hold values from 0.05 to 1
- cell_voxel: int32 [65536], P(('grp', 'gz', 'gy')), parts along dimension 0, may hold values from 0 to 4095
- block_dest: int32 [512, 1], P(('grp', 'gz', 'gy')), parts along dimension 0, may hold values from 0 to 3; in each aligned block of 32 rows (0 to 31, 32 to 63, ...) at most 24 rows name the same one
Outputs:
- new_field: float32 [8, 32, 16, 128], P('sa', ('grp', 'gz'), 'gy'), parts along dimension 1
- cell_conc: float32 [8, 65536], P('sa', ('grp', 'gz', 'gy')), parts along dimension 1
There are 2 independent parts, one for each index of `grp`. A program takes and returns all parts, laid end to end along the dimension named above; an argument that names none is the same for every part. Nothing has to cross between parts.
Inputs may be any that keep to these rules, and one draw needn't show every extreme that they name: `block_dest`: among the 32 blocks of one device at most 24 name the same destination, and in every draw some device has exactly 24 blocks naming one destination.
All inputs are finite; a program needn't handle non-finite values.
Results may differ from a plain program's by a relative error of at most 0.00007.
Values sent between devices are 32-bit elements; how exact they have to be, the bound alone decides.
A program may use at most 64 MiB of HBM per device.

v0:
```python
import math
import jax
import jax.numpy as jnp
from jax import lax
from jax.sharding import PartitionSpec as P

HIGH = lax.Precision.HIGHEST


def extended(block, sides, width):
    for axis, dim in sides:
        count = lax.axis_size(axis)
        forward = [(i, i + 1) for i in range(count - 1)]
        backward = [(target, source) for source, target in forward]
        low = lax.ppermute(
            lax.slice_in_dim(block, block.shape[dim] - width, None, axis=dim), axis, forward
        )
        high = lax.ppermute(lax.slice_in_dim(block, 0, width, axis=dim), axis, backward)
        block = jnp.concatenate([low, block, high], axis=dim)
    return block


def neighbours(padded):
    beside_all = padded[:, 2:, 1:-1, 1:-1] + padded[:, :-2, 1:-1, 1:-1]
    beside_all = beside_all + padded[:, 1:-1, 2:, 1:-1] + padded[:, 1:-1, :-2, 1:-1]
    return beside_all + padded[:, 1:-1, 1:-1, 2:] + padded[:, 1:-1, 1:-1, :-2]


def diffuse(field, diffusion):
    padded = extended(field, (("gz", 1), ("gy", 2)), 1)
    padded = jnp.pad(padded, ((0, 0), (0, 0), (0, 0), (1, 1)))
    return field + diffusion[:, None, None, None] * (neighbours(padded) - 6.0 * field)


def group_size(block_count, per_block):
    return math.gcd(block_count, max(1, 512 // per_block))


def one_hots(voxel_group, highs, lanes):
    high_ids = jnp.arange(highs, dtype=jnp.int32)
    lane_ids = jnp.arange(lanes, dtype=jnp.int32)
    onehot_high = ((voxel_group // lanes)[..., None] == high_ids).astype(jnp.float32)
    onehot_low = ((voxel_group % lanes)[..., None] == lane_ids).astype(jnp.float32)
    return (onehot_high, onehot_low)


def block_sums(values, voxel, highs, lanes, combine, init):
    quantities, block_count, per_block = values.shape
    group = group_size(block_count, per_block)
    steps_count = block_count // group
    grouped_vals = values.reshape(quantities, steps_count, group, per_block).transpose(1, 0, 2, 3)
    grouped_vox = voxel.reshape(steps_count, group, per_block)

    def step(carry, item):
        vals_group, vox_group, step_id = item
        onehot_high, onehot_low = one_hots(vox_group, highs, lanes)
        weighted = vals_group[:, :, :, None] * onehot_low[None]
        part = jnp.einsum("gch,qgcl->gqhl", onehot_high, weighted, precision=HIGH)
        return (combine(carry, part, step_id * group, group), None)

    result, unused = lax.scan(
        step, init, (grouped_vals, grouped_vox, jnp.arange(steps_count, dtype=jnp.int32))
    )
    return result


def block_reads(table_for, voxel, substrates, highs, lanes):
    block_count, per_block = voxel.shape
    group = group_size(block_count, per_block)
    steps_count = block_count // group
    grouped_vox = voxel.reshape(steps_count, group, per_block)

    def step(carry, item):
        vox_group, step_id = item
        onehot_high, onehot_low = one_hots(vox_group, highs, lanes)
        table = table_for(step_id * group, group)
        picked = jnp.einsum("gch,shl->gscl", onehot_high, table, precision=HIGH)
        return (carry, jnp.sum(picked * onehot_low[:, None], axis=3))

    unused, reads = lax.scan(step, 0, (grouped_vox, jnp.arange(steps_count, dtype=jnp.int32)))
    return reads.transpose(2, 0, 1, 3).reshape(substrates, block_count, per_block)


def deposit(secrete, uptake, cell_voxel, block_dest, voxels, lanes):
    substrates = secrete.shape[0]
    blocks = block_dest.shape[0]
    per_block = secrete.shape[1] // blocks
    highs = voxels // lanes
    slab_count = lax.axis_size("gz")
    targets = block_dest[:, 0]
    voxel_blocks = cell_voxel.reshape(blocks, per_block)
    capacity = max(2, 3 * blocks // slab_count)
    block_ids = jnp.arange(blocks, dtype=jnp.int32)
    matches = targets[:, None] == targets[None, :]
    earlier = block_ids[None, :] < block_ids[:, None]
    slot_index = jnp.sum((matches & earlier).astype(jnp.int32), axis=1)
    position = targets * capacity + slot_index
    slots = slab_count * capacity
    placing = (jnp.arange(slots, dtype=jnp.int32)[:, None] == position[None, :]).astype(jnp.float32)
    send_release = jnp.einsum(
        "pb,sbc->spc", placing, secrete.reshape(substrates, blocks, per_block), precision=HIGH
    )
    send_uptake = jnp.einsum(
        "pb,sbc->spc", placing, uptake.reshape(substrates, blocks, per_block), precision=HIGH
    )
    send_index = jnp.dot(placing, voxel_blocks.astype(jnp.float32), precision=HIGH)
    send_index = send_index.astype(jnp.int32).reshape(1, slots, per_block)
    got_release, got_uptake, got_index = (
        lax.all_to_all(send_release, "gz", split_axis=1, concat_axis=1, tiled=True),
        lax.all_to_all(send_uptake, "gz", split_axis=1, concat_axis=1, tiled=True),
        lax.all_to_all(send_index, "gz", split_axis=1, concat_axis=1, tiled=True),
    )
    slot_voxel = got_index.reshape(slots, per_block)
    stacked = jnp.concatenate([got_release, got_uptake], axis=0)

    def add_all(carry, part, first, count):
        return carry + jnp.sum(part, axis=0)

    init = jnp.zeros((2 * substrates, highs, lanes), jnp.float32)
    summed = block_sums(stacked, slot_voxel, highs, lanes, add_all, init).reshape(
        2 * substrates, voxels
    )
    source = summed[:substrates]
    uptake_sum = summed[substrates:]

    def reader(updated):
        table = updated.reshape(substrates, highs, lanes)
        looked_up = block_reads(lambda first, count: table, slot_voxel, substrates, highs, lanes)
        returned = lax.all_to_all(looked_up, "gz", split_axis=1, concat_axis=1, tiled=True)
        back = jnp.einsum("pb,spc->sbc", placing, returned, precision=HIGH)
        return back.reshape(substrates, blocks * per_block)

    return (source, uptake_sum, reader)


def shards(field, diffusion, secrete, uptake, cell_voxel, block_dest):
    substrates = field.shape[0]
    lanes = field.shape[3]
    voxels = field.shape[1] * field.shape[2] * lanes
    source, uptake_sum, reader = deposit(secrete, uptake, cell_voxel, block_dest, voxels, lanes)
    diffused = diffuse(field, diffusion).reshape(substrates, voxels)
    updated = (diffused + source) / (1.0 + uptake_sum)
    cell_conc = reader(updated)
    return (updated.reshape(field.shape), cell_conc)


def solution(mesh):
    in_specs = (
        P("sa", ("grp", "gz"), "gy", None),
        P("sa"),
        P("sa", ("grp", "gz", "gy")),
        P("sa", ("grp", "gz", "gy")),
        P(("grp", "gz", "gy")),
        P(("grp", "gz", "gy"), None),
    )
    out_specs = (P("sa", ("grp", "gz"), "gy", None), P("sa", ("grp", "gz", "gy")))
    return jax.shard_map(shards, mesh=mesh, in_specs=in_specs, out_specs=out_specs, check_vma=False)
```

profile of v0, /device:TPU:0, one launch (start us, length us, event | category | flops | bytes accessed | tf_op | source)
XLA Modules:
  0.0 118.7 jit_solution(11826581008800157441)
XLA Ops:
  2.2 1.2 %convolution_bitcast_fusion = f32[4,96,128]{2,1,0:T(8,128)S(1)} fusion(f32[1,4,32,128]{3,1,2,0:T(4,128)} %bitcast.137, s32[32]{0:T(128)S(1)} %multiply_add_fusion), kind=kOutput, calls=%fused_computation.41 | convolution fusion | flops 18877440 | bytes 262272 | tf_op jit(solution)/shard_map/pb,sbc->spc/dot_general | solution.py:103
  4.2 6.3 %all-to-all-start.1 = ((f32[4,96,128]{2,0,1:T(4,128)}), f32[4,96,128]{2,0,1:T(4,128)S(1)}, u32[]{:S(2)}, u32[]{:S(2)}) async-start(f32[4,96,128]{2,0,1:T(4,128)} %copy.16), calls=%async_computation.1 | async-start | bytes 393216 | tf_op jit(solution)/shard_map/all_to_all | solution.py:110
  10.6 3.9 %collective-permute-start.1 = (f32[4,1,8,128]{3,2,1,0:T(8,128)S(1)}, f32[4,1,8,128]{3,2,1,0:T(8,128)S(1)}, u32[]{:S(2)}, u32[]{:S(2)}) collective-permute-start(f32[4,1,8,128]{3,2,1,0:T(8,128)S(1)} %get-tuple-element.156), channel_id=1, source_target_pairs={{0,4},{4,8},{8,12},{1,5},{5,9},{9,13},{2,6},{6,10},{10,14},{3,7},{... | collective-permute-start | bytes 49160 | tf_op jit(solution)/shard_map/ppermute | solution.py:15
  14.5 1.3 %collective-permute-start = (f32[4,1,8,128]{3,2,1,0:T(8,128)S(1)}, f32[4,1,8,128]{3,2,1,0:T(8,128)S(1)}, u32[]{:S(2)}, u32[]{:S(2)}) collective-permute-start(f32[4,1,8,128]{3,2,1,0:T(8,128)S(1)} %get-tuple-element.155), channel_id=1, source_target_pairs={{4,0},{8,4},{12,8},{5,1},{9,5},{13,9},{6,2},{10,6},{14,10},{7,3},{... | collective-permute-start | bytes 49160 | tf_op jit(solution)/shard_map/ppermute | solution.py:18
  17.0 3.1 %collective-permute-done = f32[4,1,8,128]{3,2,1,0:T(8,128)S(1)} collective-permute-done((f32[4,1,8,128]{3,2,1,0:T(8,128)S(1)}, f32[4,1,8,128]{3,2,1,0:T(8,128)S(1)}, u32[]{:S(2)}, u32[]{:S(2)}) %collective-permute-start) | collective-permute-done | bytes 16416 | tf_op jit(solution)/shard_map/ppermute | solution.py:18
  20.2 1.3 %collective-permute-start.2 = (f32[4,6,1,128]{3,2,1,0:T(1,128)S(1)}, f32[4,6,1,128]{3,2,1,0:T(1,128)S(1)}, u32[]{:S(2)}, u32[]{:S(2)}) collective-permute-start(f32[4,6,1,128]{3,2,1,0:T(1,128)S(1)} %get-tuple-element.154), channel_id=1, source_target_pairs={{2,0},{3,1},{6,4},{7,5},{10,8},{11,9},{14,12},{15,13},{18,16},{19,... | collective-permute-start | bytes 36872 | tf_op jit(solution)/shard_map/ppermute | solution.py:18
  21.5 4.5 %collective-permute-start.3 = (f32[4,6,1,128]{3,2,1,0:T(1,128)S(1)}, f32[4,6,1,128]{3,2,1,0:T(1,128)S(1)}, u32[]{:S(2)}, u32[]{:S(2)}) collective-permute-start(f32[4,6,1,128]{3,2,1,0:T(1,128)S(1)} %get-tuple-element.153), channel_id=1, source_target_pairs={{0,2},{1,3},{4,6},{5,7},{8,10},{9,11},{12,14},{13,15},{16,18},{17,... | collective-permute-start | bytes 36872 | tf_op jit(solution)/shard_map/ppermute | solution.py:15
  26.0 3.6 %all-to-all-start = ((f32[4,96,128]{2,0,1:T(4,128)}), f32[4,96,128]{2,0,1:T(4,128)S(1)}, u32[]{:S(2)}, u32[]{:S(2)}) async-start(f32[4,96,128]{2,0,1:T(4,128)} %copy.15), calls=%async_computation | async-start | bytes 393216 | tf_op jit(solution)/shard_map/all_to_all | solution.py:109
  30.9 5.0 %all-to-all-done = f32[4,96,128]{2,0,1:T(4,128)S(1)} async-done(((f32[4,96,128]{2,0,1:T(4,128)}), f32[4,96,128]{2,0,1:T(4,128)S(1)}, u32[]{:S(2)}, u32[]{:S(2)}) %all-to-all-start) | async-done | bytes 196640 | tf_op jit(solution)/shard_map/all_to_all | solution.py:109
  35.9 3.3 %all-to-all-start.2 = ((s32[1,96,128]{2,0,1:T(1,128)}), s32[1,96,128]{2,0,1:T(1,128)S(1)}, u32[]{:S(2)}, u32[]{:S(2)}) async-start(s32[1,96,128]{2,0,1:T(1,128)} %bitcast.14), calls=%async_computation.2 | async-start | bytes 98304 | tf_op jit(solution)/shard_map/all_to_all | solution.py:111
  39.4 5.5 %all-to-all-done.2 = s32[1,96,128]{2,0,1:T(1,128)S(1)} async-done(((s32[1,96,128]{2,0,1:T(1,128)}), s32[1,96,128]{2,0,1:T(1,128)S(1)}, u32[]{:S(2)}, u32[]{:S(2)}) %all-to-all-start.2) | async-done | bytes 49184 | tf_op jit(solution)/shard_map/all_to_all | solution.py:111
  44.9 31.3 %while.26 = (s32[]{:T(128)}, f32[8,32,128]{2,1,0:T(8,128)S(1)}, f32[24,8,4,128]{3,2,1,0:T(4,128)S(1)}, s32[24,4,128]{2,1,0:T(4,128)S(1)}, s32[]{:T(128)}, /*index=5*/s32[]{:T(128)}) while((s32[]{:T(128)}, f32[8,32,128]{2,1,0:T(8,128)S(1)}, f32[24,8,4,128]{3,2,1,0:T(4,128)S(1)}, s32[24,4,128]{2,1,0:T(4,128)S(1)}, s32[]{:T(128)}, ...), condition=%wide.region_2.3_spmd.clone, body=%wide.region_1.2_spmd.clone.sunk | while | flops 202073600 | bytes 845919 | solution.py:61
  46.4 1.1 fusion.66
  47.7 1.1 fusion.66
  50.3 1.1 fusion.66
  51.6 1.1 fusion.66
  52.9 1.1 fusion.66
  54.2 1.1 fusion.66
  56.8 1.1 fusion.66
  58.1 1.1 fusion.66
  59.4 1.1 fusion.66
  60.7 1.1 fusion.66
  63.3 1.1 fusion.66
  64.6 1.1 fusion.66
  65.9 1.1 fusion.66
  67.2 1.1 fusion.66
  69.8 1.1 fusion.66
  71.1 1.1 fusion.66
  72.4 1.1 fusion.66
  76.3 31.9 %while.25 = (s32[]{:T(128)}, f32[24,4,4,128]{3,2,1,0:T(4,128)}, s32[24,4,128]{2,1,0:T(4,128)S(1)}, f32[4,32,128]{2,1,0:T(8,128)S(1)}, s32[]{:T(128)}) while((s32[]{:T(128)}, f32[24,4,4,128]{3,2,1,0:T(4,128)}, s32[24,4,128]{2,1,0:T(4,128)S(1)}, f32[4,32,128]{2,1,0:T(8,128)S(1)}, s32[]{:T(128)}) %tuple.72), condition=%wide.region_5.6_spmd, body=%wide.region_3.5_spmd.sunk | while | flops 101342720 | bytes 624717 | solution.py:80
  108.2 3.4 %all-to-all-start.3 = ((f32[4,96,128]{2,0,1:T(4,128)}), f32[4,96,128]{2,0,1:T(4,128)S(1)}, u32[]{:S(2)}, u32[]{:S(2)}) async-start(f32[4,96,128]{2,0,1:T(4,128)} %bitcast.20), calls=%async_computation.3 | async-start | bytes 393216 | tf_op jit(solution)/shard_map/all_to_all | solution.py:129
  112.2 5.6 %all-to-all-done.3 = f32[4,96,128]{2,0,1:T(4,128)S(1)} async-done(((f32[4,96,128]{2,0,1:T(4,128)}), f32[4,96,128]{2,0,1:T(4,128)S(1)}, u32[]{:S(2)}, u32[]{:S(2)}) %all-to-all-start.3) | async-done | bytes 196640 | tf_op jit(solution)/shard_map/all_to_all | solution.py:129
  (207 shorter events, 49.7 us)
Async XLA Ops:
  3.4 7.2 %copy-start = (f32[4,4,8,128]{3,2,1,0:T(8,128)S(1)}, f32[4,4,8,128]{3,2,1,0:T(8,128)}, u32[]{:S(2)}) copy-start(f32[4,4,8,128]{3,2,1,0:T(8,128)} %param.10) | copy-start | bytes 196612
  3.4 12.4 %copy-start.1 = (f32[4,4096]{1,0:T(4,128)S(1)}, f32[4,4096]{1,0:T(4,128)}, u32[]{:S(2)}) copy-start(f32[4,4096]{1,0:T(4,128)} %param.12) | copy-start | bytes 196612
  4.2 21.8 %all-to-all-start.1 = ((f32[4,96,128]{2,0,1:T(4,128)}), f32[4,96,128]{2,0,1:T(4,128)S(1)}, u32[]{:S(2)}, u32[]{:S(2)}) async-start(f32[4,96,128]{2,0,1:T(4,128)} %copy.16), calls=%async_computation.1 | async-start | bytes 393216 | tf_op jit(solution)/shard_map/all_to_all | solution.py:110
  10.6 6.4 %collective-permute-start.1 = (f32[4,1,8,128]{3,2,1,0:T(8,128)S(1)}, f32[4,1,8,128]{3,2,1,0:T(8,128)S(1)}, u32[]{:S(2)}, u32[]{:S(2)}) collective-permute-start(f32[4,1,8,128]{3,2,1,0:T(8,128)S(1)} %get-tuple-element.156), channel_id=1, source_target_pairs={{0,4},{4,8},{8,12},{1,5},{5,9},{9,13},{2,6},{6,10},{10,14},{3,7},{... | collective-permute-start | bytes 49160 | tf_op jit(solution)/shard_map/ppermute | solution.py:15
  14.5 5.6 %collective-permute-start = (f32[4,1,8,128]{3,2,1,0:T(8,128)S(1)}, f32[4,1,8,128]{3,2,1,0:T(8,128)S(1)}, u32[]{:S(2)}, u32[]{:S(2)}) collective-permute-start(f32[4,1,8,128]{3,2,1,0:T(8,128)S(1)} %get-tuple-element.155), channel_id=1, source_target_pairs={{4,0},{8,4},{12,8},{5,1},{9,5},{13,9},{6,2},{10,6},{14,10},{7,3},{... | collective-permute-start | bytes 49160 | tf_op jit(solution)/shard_map/ppermute | solution.py:18
  17.0 12.7 %copy-start.2 = (s32[4096]{0:T(1024)S(1)}, s32[4096]{0:T(1024)}, u32[]{:S(2)}) copy-start(s32[4096]{0:T(1024)} %param.14) | copy-start | bytes 49156
  20.2 10.4 %collective-permute-start.2 = (f32[4,6,1,128]{3,2,1,0:T(1,128)S(1)}, f32[4,6,1,128]{3,2,1,0:T(1,128)S(1)}, u32[]{:S(2)}, u32[]{:S(2)}) collective-permute-start(f32[4,6,1,128]{3,2,1,0:T(1,128)S(1)} %get-tuple-element.154), channel_id=1, source_target_pairs={{2,0},{3,1},{6,4},{7,5},{10,8},{11,9},{14,12},{15,13},{18,16},{19,... | collective-permute-start | bytes 36872 | tf_op jit(solution)/shard_map/ppermute | solution.py:18
  21.5 9.1 %collective-permute-start.3 = (f32[4,6,1,128]{3,2,1,0:T(1,128)S(1)}, f32[4,6,1,128]{3,2,1,0:T(1,128)S(1)}, u32[]{:S(2)}, u32[]{:S(2)}) collective-permute-start(f32[4,6,1,128]{3,2,1,0:T(1,128)S(1)} %get-tuple-element.153), channel_id=1, source_target_pairs={{0,2},{1,3},{4,6},{5,7},{8,10},{9,11},{12,14},{13,15},{16,18},{17,... | collective-permute-start | bytes 36872 | tf_op jit(solution)/shard_map/ppermute | solution.py:15
  26.0 9.9 %all-to-all-start = ((f32[4,96,128]{2,0,1:T(4,128)}), f32[4,96,128]{2,0,1:T(4,128)S(1)}, u32[]{:S(2)}, u32[]{:S(2)}) async-start(f32[4,96,128]{2,0,1:T(4,128)} %copy.15), calls=%async_computation | async-start | bytes 393216 | tf_op jit(solution)/shard_map/all_to_all | solution.py:109
  35.9 8.9 %all-to-all-start.2 = ((s32[1,96,128]{2,0,1:T(1,128)}), s32[1,96,128]{2,0,1:T(1,128)S(1)}, u32[]{:S(2)}, u32[]{:S(2)}) async-start(s32[1,96,128]{2,0,1:T(1,128)} %bitcast.14), calls=%async_computation.2 | async-start | bytes 98304 | tf_op jit(solution)/shard_map/all_to_all | solution.py:111
  44.9 31.3 %copy-start.3 = (f32[4]{0:T(128)S(1)}, f32[4]{0:T(128)}, u32[]{:S(2)}) copy-start(f32[4]{0:T(128)} %param.11) | copy-start | bytes 52
  108.2 9.6 %all-to-all-start.3 = ((f32[4,96,128]{2,0,1:T(4,128)}), f32[4,96,128]{2,0,1:T(4,128)S(1)}, u32[]{:S(2)}, u32[]{:S(2)}) async-start(f32[4,96,128]{2,0,1:T(4,128)} %bitcast.20), calls=%async_computation.3 | async-start | bytes 393216 | tf_op jit(solution)/shard_map/all_to_all | solution.py:129
where the time goes:
time: 119 us
  matrix products  45.3 us (38%)
  starting transfers between devices  27.7 us (23%)
  waiting for transfers between devices  19.2 us (16%)
  local copies, waits for them, and re-layouts  17.1 us (14%)
  other arithmetic  7.06 us (6%)
  loops' own time  1.48 us (1%)
    dot_general x24, matrix products, step(): part = jnp.einsum('gch,qgcl->gqhl', onehot_high, weighted, precision=HIGH)  26.3 us
    dot_general x24, matrix products, step(): picked = jnp.einsum('gch,shl->gscl', onehot_high, table, precision=HIGH)  16.3 us
    dynamic_update_slice x24, local copies, waits for them, and re-layouts, block_reads(): lax.scan(step, 0, (grouped_vox, jnp.arange(steps_count, dtype=jnp.int32)))  14.4 us
    ppermute x2, starting transfers between devices, extended(): lax.ppermute(lax.slice_in_dim(block, block.shape[dim] - width, None, axis...  8.46 us
    all_to_all x1, starting transfers between devices, deposit(): lax.all_to_all(send_uptake, 'gz', split_axis=1, concat_axis=1, tiled=True)  6.35 us
    all_to_all x1, waiting for transfers between devices, reader(): lax.all_to_all(looked_up, 'gz', split_axis=1, concat_axis=1, tiled=True)  5.57 us
    all_to_all x1, waiting for transfers between devices, deposit(): lax.all_to_all(send_index, 'gz', split_axis=1, concat_axis=1, tiled=True)  5.47 us
    all_to_all x1, waiting for transfers between devices, deposit(): lax.all_to_all(send_release, 'gz', split_axis=1, concat_axis=1, tiled=True)  5.03 us
  transfers between devices with their start and end apart: 8, of which 4 were waited for; matrix products, arithmetic and copies ran while one was open for 3% of the time, Pallas kernels for 0%

commit v1 on v0

--- a/solution.py
+++ b/solution.py
@@ -126,7 +126,12 @@
     def reader(updated):
         table = updated.reshape(substrates, highs, lanes)
         looked_up = block_reads(lambda first, count: table, slot_voxel, substrates, highs, lanes)
-        returned = lax.all_to_all(looked_up, "gz", split_axis=1, concat_axis=1, tiled=True)
+        returned = jnp.concatenate(
+            lax.all_to_all(
+                jnp.stack(jnp.split(looked_up, lax.axis_size("gz"), axis=1)), "gz", 0, 0
+            ),
+            axis=1,
+        )
         back = jnp.einsum("pb,spc->sbc", placing, returned, precision=HIGH)
         return back.reshape(substrates, blocks * per_block)
 

time: 119 us -> 107 us (0.90)
  local copies, waits for them, and re-layouts: 17.1 us -> 3.11 us
    dynamic_update_slice x24, local copies, waits for them, and re-layouts: 14.4 us -> 0.32 us  [block_reads(): lax.scan(step, 0, (grouped_vox, jnp.arange(steps_count, dtype=jnp.int32)))]
where the time goes in v1:
time: 107 us; the launch traced here: 106 us
  matrix products  45.4 us (42%)
  starting transfers between devices  27.7 us (26%)
  waiting for transfers between devices  19.2 us (18%)
  other arithmetic  7.86 us (7%)
  local copies, waits for them, and re-layouts  3.11 us (3%)
  loops' own time  2.03 us (2%)
    dot_general x24, matrix products, step(): part = jnp.einsum('gch,qgcl->gqhl', onehot_high, weighted, precision=HIGH)  26.3 us
    dot_general x24, matrix products, step(): picked = jnp.einsum('gch,shl->gscl', onehot_high, table, precision=HIGH)  16.4 us
    ppermute x2, starting transfers between devices, extended(): lax.ppermute(lax.slice_in_dim(block, block.shape[dim] - width, None, axis...  8.46 us
    all_to_all x1, starting transfers between devices, deposit(): lax.all_to_all(send_uptake, 'gz', split_axis=1, concat_axis=1, tiled=True)  6.35 us
    all_to_all x1, waiting for transfers between devices, reader(): lax.all_to_all(jnp.stack(jnp.split(looked_up, lax.axis_size('gz'), axis=1...  5.57 us
    all_to_all x1, waiting for transfers between devices, deposit(): lax.all_to_all(send_index, 'gz', split_axis=1, concat_axis=1, tiled=True)  5.47 us
    all_to_all x1, waiting for transfers between devices, deposit(): lax.all_to_all(send_release, 'gz', split_axis=1, concat_axis=1, tiled=True)  5.03 us
    convert_element_type x48, other arithmetic, one_hots(): ((voxel_group % lanes)[..., None] == lane_ids).astype(jnp.float32)  3.73 us
  transfers between devices with their start and end apart: 8, of which 4 were waited for; matrix products, arithmetic and copies ran while one was open for 3% of the time, Pallas kernels for 0%

profile of v1, /device:TPU:0, one launch (start us, length us, event | category | flops | bytes accessed | tf_op | source)
XLA Modules:
  0.0 106.1 jit_solution(1486302032031391422)
XLA Ops:
  2.2 1.2 %convolution_bitcast_fusion = f32[4,96,128]{2,1,0:T(8,128)S(1)} fusion(f32[1,4,32,128]{3,1,2,0:T(4,128)} %bitcast.151, s32[32]{0:T(128)S(1)} %multiply_add_fusion), kind=kOutput, calls=%fused_computation.41 | convolution fusion | flops 18877440 | bytes 262272 | tf_op jit(solution)/shard_map/pb,sbc->spc/dot_general | solution.py:103
  4.2 6.3 %all-to-all-start.1 = ((f32[4,96,128]{2,0,1:T(4,128)}), f32[4,96,128]{2,0,1:T(4,128)S(1)}, u32[]{:S(2)}, u32[]{:S(2)}) async-start(f32[4,96,128]{2,0,1:T(4,128)} %copy.20), calls=%async_computation.1 | async-start | bytes 393216 | tf_op jit(solution)/shard_map/all_to_all | solution.py:110
  10.6 3.9 %collective-permute-start.1 = (f32[4,1,8,128]{3,2,1,0:T(8,128)S(1)}, f32[4,1,8,128]{3,2,1,0:T(8,128)S(1)}, u32[]{:S(2)}, u32[]{:S(2)}) collective-permute-start(f32[4,1,8,128]{3,2,1,0:T(8,128)S(1)} %get-tuple-element.160), channel_id=1, source_target_pairs={{0,4},{4,8},{8,12},{1,5},{5,9},{9,13},{2,6},{6,10},{10,14},{3,7},{... | collective-permute-start | bytes 49160 | tf_op jit(solution)/shard_map/ppermute | solution.py:15
  14.5 1.3 %collective-permute-start = (f32[4,1,8,128]{3,2,1,0:T(8,128)S(1)}, f32[4,1,8,128]{3,2,1,0:T(8,128)S(1)}, u32[]{:S(2)}, u32[]{:S(2)}) collective-permute-start(f32[4,1,8,128]{3,2,1,0:T(8,128)S(1)} %get-tuple-element.159), channel_id=1, source_target_pairs={{4,0},{8,4},{12,8},{5,1},{9,5},{13,9},{6,2},{10,6},{14,10},{7,3},{... | collective-permute-start | bytes 49160 | tf_op jit(solution)/shard_map/ppermute | solution.py:18
  17.0 3.1 %collective-permute-done = f32[4,1,8,128]{3,2,1,0:T(8,128)S(1)} collective-permute-done((f32[4,1,8,128]{3,2,1,0:T(8,128)S(1)}, f32[4,1,8,128]{3,2,1,0:T(8,128)S(1)}, u32[]{:S(2)}, u32[]{:S(2)}) %collective-permute-start) | collective-permute-done | bytes 16416 | tf_op jit(solution)/shard_map/ppermute | solution.py:18
  20.2 1.3 %collective-permute-start.2 = (f32[4,6,1,128]{3,2,1,0:T(1,128)S(1)}, f32[4,6,1,128]{3,2,1,0:T(1,128)S(1)}, u32[]{:S(2)}, u32[]{:S(2)}) collective-permute-start(f32[4,6,1,128]{3,2,1,0:T(1,128)S(1)} %get-tuple-element.158), channel_id=1, source_target_pairs={{2,0},{3,1},{6,4},{7,5},{10,8},{11,9},{14,12},{15,13},{18,16},{19,... | collective-permute-start | bytes 36872 | tf_op jit(solution)/shard_map/ppermute | solution.py:18
  21.5 4.5 %collective-permute-start.3 = (f32[4,6,1,128]{3,2,1,0:T(1,128)S(1)}, f32[4,6,1,128]{3,2,1,0:T(1,128)S(1)}, u32[]{:S(2)}, u32[]{:S(2)}) collective-permute-start(f32[4,6,1,128]{3,2,1,0:T(1,128)S(1)} %get-tuple-element.157), channel_id=1, source_target_pairs={{0,2},{1,3},{4,6},{5,7},{8,10},{9,11},{12,14},{13,15},{16,18},{17,... | collective-permute-start | bytes 36872 | tf_op jit(solution)/shard_map/ppermute | solution.py:15
  26.0 3.6 %all-to-all-start = ((f32[4,96,128]{2,0,1:T(4,128)}), f32[4,96,128]{2,0,1:T(4,128)S(1)}, u32[]{:S(2)}, u32[]{:S(2)}) async-start(f32[4,96,128]{2,0,1:T(4,128)} %copy.19), calls=%async_computation | async-start | bytes 393216 | tf_op jit(solution)/shard_map/all_to_all | solution.py:109
  30.9 5.0 %all-to-all-done = f32[4,96,128]{2,0,1:T(4,128)S(1)} async-done(((f32[4,96,128]{2,0,1:T(4,128)}), f32[4,96,128]{2,0,1:T(4,128)S(1)}, u32[]{:S(2)}, u32[]{:S(2)}) %all-to-all-start) | async-done | bytes 196640 | tf_op jit(solution)/shard_map/all_to_all | solution.py:109
  35.9 3.3 %all-to-all-start.2 = ((s32[1,96,128]{2,0,1:T(1,128)}), s32[1,96,128]{2,0,1:T(1,128)S(1)}, u32[]{:S(2)}, u32[]{:S(2)}) async-start(s32[1,96,128]{2,0,1:T(1,128)} %bitcast.14), calls=%async_computation.2 | async-start | bytes 98304 | tf_op jit(solution)/shard_map/all_to_all | solution.py:111
  39.4 5.5 %all-to-all-done.2 = s32[1,96,128]{2,0,1:T(1,128)S(1)} async-done(((s32[1,96,128]{2,0,1:T(1,128)}), s32[1,96,128]{2,0,1:T(1,128)S(1)}, u32[]{:S(2)}, u32[]{:S(2)}) %all-to-all-start.2) | async-done | bytes 49184 | tf_op jit(solution)/shard_map/all_to_all | solution.py:111
  44.9 31.3 %while.26 = (s32[]{:T(128)}, f32[8,32,128]{2,1,0:T(8,128)S(1)}, f32[24,8,4,128]{3,2,1,0:T(4,128)S(1)}, s32[24,4,128]{2,1,0:T(4,128)S(1)}, s32[]{:T(128)}, /*index=5*/s32[]{:T(128)}) while((s32[]{:T(128)}, f32[8,32,128]{2,1,0:T(8,128)S(1)}, f32[24,8,4,128]{3,2,1,0:T(4,128)S(1)}, s32[24,4,128]{2,1,0:T(4,128)S(1)}, s32[]{:T(128)}, ...), condition=%wide.region_2.3_spmd.clone, body=%wide.region_1.2_spmd.clone.sunk | while | flops 202073600 | bytes 845919 | solution.py:61
  46.4 1.1 %fusion.66 = f32[8,32,128]{2,1,0:T(8,128)S(1)} fusion(f32[4,128,128]{2,1,0:T(8,128)S(1)} %fusion.65, f32[8,4,128]{2,1,0:T(4,128)S(1)} %dynamic-slice_bitcast_fusion.2, f32[8,32,128]{2,1,0:T(8,128)S(1)} %get-tuple-element.226, pred[]{:T(512)S(6)} %compare.42, s32[4,128]{1,0:T(4,128)S(1)} %get-tuple-element.218), kind=kOutput, calls=%fused_computation.22.clone.1 | convolution fusion | flops 201932800 | bytes 542721 | tf_op jit(solution)/shard_map/while/body/eval_jaxpr/gch,qgcl->gqhl/dot_general | solution.py:58
  47.7 1.1 %fusion.66 = f32[8,32,128]{2,1,0:T(8,128)S(1)} fusion(f32[4,128,128]{2,1,0:T(8,128)S(1)} %fusion.65, f32[8,4,128]{2,1,0:T(4,128)S(1)} %dynamic-slice_bitcast_fusion.2, f32[8,32,128]{2,1,0:T(8,128)S(1)} %get-tuple-element.226, pred[]{:T(512)S(6)} %compare.42, s32[4,128]{1,0:T(4,128)S(1)} %get-tuple-element.218), kind=kOutput, calls=%fused_computation.22.clone.1 | convolution fusion | flops 201932800 | bytes 542721 | tf_op jit(solution)/shard_map/while/body/eval_jaxpr/gch,qgcl->gqhl/dot_general | solution.py:58
  49.0 1.1 %fusion.66 = f32[8,32,128]{2,1,0:T(8,128)S(1)} fusion(f32[4,128,128]{2,1,0:T(8,128)S(1)} %fusion.65, f32[8,4,128]{2,1,0:T(4,128)S(1)} %dynamic-slice_bitcast_fusion.2, f32[8,32,128]{2,1,0:T(8,128)S(1)} %get-tuple-element.226, pred[]{:T(512)S(6)} %compare.42, s32[4,128]{1,0:T(4,128)S(1)} %get-tuple-element.218), kind=kOutput, calls=%fused_computation.22.clone.1 | convolution fusion | flops 201932800 | bytes 542721 | tf_op jit(solution)/shard_map/while/body/eval_jaxpr/gch,qgcl->gqhl/dot_general | solution.py:58
  50.3 1.1 %fusion.66 = f32[8,32,128]{2,1,0:T(8,128)S(1)} fusion(f32[4,128,128]{2,1,0:T(8,128)S(1)} %fusion.65, f32[8,4,128]{2,1,0:T(4,128)S(1)} %dynamic-slice_bitcast_fusion.2, f32[8,32,128]{2,1,0:T(8,128)S(1)} %get-tuple-element.226, pred[]{:T(512)S(6)} %compare.42, s32[4,128]{1,0:T(4,128)S(1)} %get-tuple-element.218), kind=kOutput, calls=%fused_computation.22.clone.1 | convolution fusion | flops 201932800 | bytes 542721 | tf_op jit(solution)/shard_map/while/body/eval_jaxpr/gch,qgcl->gqhl/dot_general | solution.py:58
  52.9 1.1 %fusion.66 = f32[8,32,128]{2,1,0:T(8,128)S(1)} fusion(f32[4,128,128]{2,1,0:T(8,128)S(1)} %fusion.65, f32[8,4,128]{2,1,0:T(4,128)S(1)} %dynamic-slice_bitcast_fusion.2, f32[8,32,128]{2,1,0:T(8,128)S(1)} %get-tuple-element.226, pred[]{:T(512)S(6)} %compare.42, s32[4,128]{1,0:T(4,128)S(1)} %get-tuple-element.218), kind=kOutput, calls=%fused_computation.22.clone.1 | convolution fusion | flops 201932800 | bytes 542721 | tf_op jit(solution)/shard_map/while/body/eval_jaxpr/gch,qgcl->gqhl/dot_general | solution.py:58
  54.2 1.1 %fusion.66 = f32[8,32,128]{2,1,0:T(8,128)S(1)} fusion(f32[4,128,128]{2,1,0:T(8,128)S(1)} %fusion.65, f32[8,4,128]{2,1,0:T(4,128)S(1)} %dynamic-slice_bitcast_fusion.2, f32[8,32,128]{2,1,0:T(8,128)S(1)} %get-tuple-element.226, pred[]{:T(512)S(6)} %compare.42, s32[4,128]{1,0:T(4,128)S(1)} %get-tuple-element.218), kind=kOutput, calls=%fused_computation.22.clone.1 | convolution fusion | flops 201932800 | bytes 542721 | tf_op jit(solution)/shard_map/while/body/eval_jaxpr/gch,qgcl->gqhl/dot_general | solution.py:58
  55.5 1.1 %fusion.66 = f32[8,32,128]{2,1,0:T(8,128)S(1)} fusion(f32[4,128,128]{2,1,0:T(8,128)S(1)} %fusion.65, f32[8,4,128]{2,1,0:T(4,128)S(1)} %dynamic-slice_bitcast_fusion.2, f32[8,32,128]{2,1,0:T(8,128)S(1)} %get-tuple-element.226, pred[]{:T(512)S(6)} %compare.42, s32[4,128]{1,0:T(4,128)S(1)} %get-tuple-element.218), kind=kOutput, calls=%fused_computation.22.clone.1 | convolution fusion | flops 201932800 | bytes 542721 | tf_op jit(solution)/shard_map/while/body/eval_jaxpr/gch,qgcl->gqhl/dot_general | solution.py:58
  56.8 1.1 %fusion.66 = f32[8,32,128]{2,1,0:T(8,128)S(1)} fusion(f32[4,128,128]{2,1,0:T(8,128)S(1)} %fusion.65, f32[8,4,128]{2,1,0:T(4,128)S(1)} %dynamic-slice_bitcast_fusion.2, f32[8,32,128]{2,1,0:T(8,128)S(1)} %get-tuple-element.226, pred[]{:T(512)S(6)} %compare.42, s32[4,128]{1,0:T(4,128)S(1)} %get-tuple-element.218), kind=kOutput, calls=%fused_computation.22.clone.1 | convolution fusion | flops 201932800 | bytes 542721 | tf_op jit(solution)/shard_map/while/body/eval_jaxpr/gch,qgcl->gqhl/dot_general | solution.py:58
  59.4 1.1 %fusion.66 = f32[8,32,128]{2,1,0:T(8,128)S(1)} fusion(f32[4,128,128]{2,1,0:T(8,128)S(1)} %fusion.65, f32[8,4,128]{2,1,0:T(4,128)S(1)} %dynamic-slice_bitcast_fusion.2, f32[8,32,128]{2,1,0:T(8,128)S(1)} %get-tuple-element.226, pred[]{:T(512)S(6)} %compare.42, s32[4,128]{1,0:T(4,128)S(1)} %get-tuple-element.218), kind=kOutput, calls=%fused_computation.22.clone.1 | convolution fusion | flops 201932800 | bytes 542721 | tf_op jit(solution)/shard_map/while/body/eval_jaxpr/gch,qgcl->gqhl/dot_general | solution.py:58
  60.7 1.1 %fusion.66 = f32[8,32,128]{2,1,0:T(8,128)S(1)} fusion(f32[4,128,128]{2,1,0:T(8,128)S(1)} %fusion.65, f32[8,4,128]{2,1,0:T(4,128)S(1)} %dynamic-slice_bitcast_fusion.2, f32[8,32,128]{2,1,0:T(8,128)S(1)} %get-tuple-element.226, pred[]{:T(512)S(6)} %compare.42, s32[4,128]{1,0:T(4,128)S(1)} %get-tuple-element.218), kind=kOutput, calls=%fused_computation.22.clone.1 | convolution fusion | flops 201932800 | bytes 542721 | tf_op jit(solution)/shard_map/while/body/eval_jaxpr/gch,qgcl->gqhl/dot_general | solution.py:58
  62.0 1.1 %fusion.66 = f32[8,32,128]{2,1,0:T(8,128)S(1)} fusion(f32[4,128,128]{2,1,0:T(8,128)S(1)} %fusion.65, f32[8,4,128]{2,1,0:T(4,128)S(1)} %dynamic-slice_bitcast_fusion.2, f32[8,32,128]{2,1,0:T(8,128)S(1)} %get-tuple-element.226, pred[]{:T(512)S(6)} %compare.42, s32[4,128]{1,0:T(4,128)S(1)} %get-tuple-element.218), kind=kOutput, calls=%fused_computation.22.clone.1 | convolution fusion | flops 201932800 | bytes 542721 | tf_op jit(solution)/shard_map/while/body/eval_jaxpr/gch,qgcl->gqhl/dot_general | solution.py:58
  63.3 1.1 %fusion.66 = f32[8,32,128]{2,1,0:T(8,128)S(1)} fusion(f32[4,128,128]{2,1,0:T(8,128)S(1)} %fusion.65, f32[8,4,128]{2,1,0:T(4,128)S(1)} %dynamic-slice_bitcast_fusion.2, f32[8,32,128]{2,1,0:T(8,128)S(1)} %get-tuple-element.226, pred[]{:T(512)S(6)} %compare.42, s32[4,128]{1,0:T(4,128)S(1)} %get-tuple-element.218), kind=kOutput, calls=%fused_computation.22.clone.1 | convolution fusion | flops 201932800 | bytes 542721 | tf_op jit(solution)/shard_map/while/body/eval_jaxpr/gch,qgcl->gqhl/dot_general | solution.py:58
  65.9 1.1 %fusion.66 = f32[8,32,128]{2,1,0:T(8,128)S(1)} fusion(f32[4,128,128]{2,1,0:T(8,128)S(1)} %fusion.65, f32[8,4,128]{2,1,0:T(4,128)S(1)} %dynamic-slice_bitcast_fusion.2, f32[8,32,128]{2,1,0:T(8,128)S(1)} %get-tuple-element.226, pred[]{:T(512)S(6)} %compare.42, s32[4,128]{1,0:T(4,128)S(1)} %get-tuple-element.218), kind=kOutput, calls=%fused_computation.22.clone.1 | convolution fusion | flops 201932800 | bytes 542721 | tf_op jit(solution)/shard_map/while/body/eval_jaxpr/gch,qgcl->gqhl/dot_general | solution.py:58
  67.2 1.1 %fusion.66 = f32[8,32,128]{2,1,0:T(8,128)S(1)} fusion(f32[4,128,128]{2,1,0:T(8,128)S(1)} %fusion.65, f32[8,4,128]{2,1,0:T(4,128)S(1)} %dynamic-slice_bitcast_fusion.2, f32[8,32,128]{2,1,0:T(8,128)S(1)} %get-tuple-element.226, pred[]{:T(512)S(6)} %compare.42, s32[4,128]{1,0:T(4,128)S(1)} %get-tuple-element.218), kind=kOutput, calls=%fused_computation.22.clone.1 | convolution fusion | flops 201932800 | bytes 542721 | tf_op jit(solution)/shard_map/while/body/eval_jaxpr/gch,qgcl->gqhl/dot_general | solution.py:58
  68.5 1.1 %fusion.66 = f32[8,32,128]{2,1,0:T(8,128)S(1)} fusion(f32[4,128,128]{2,1,0:T(8,128)S(1)} %fusion.65, f32[8,4,128]{2,1,0:T(4,128)S(1)} %dynamic-slice_bitcast_fusion.2, f32[8,32,128]{2,1,0:T(8,128)S(1)} %get-tuple-element.226, pred[]{:T(512)S(6)} %compare.42, s32[4,128]{1,0:T(4,128)S(1)} %get-tuple-element.218), kind=kOutput, calls=%fused_computation.22.clone.1 | convolution fusion | flops 201932800 | bytes 542721 | tf_op jit(solution)/shard_map/while/body/eval_jaxpr/gch,qgcl->gqhl/dot_general | solution.py:58
  69.8 1.1 %fusion.66 = f32[8,32,128]{2,1,0:T(8,128)S(1)} fusion(f32[4,128,128]{2,1,0:T(8,128)S(1)} %fusion.65, f32[8,4,128]{2,1,0:T(4,128)S(1)} %dynamic-slice_bitcast_fusion.2, f32[8,32,128]{2,1,0:T(8,128)S(1)} %get-tuple-element.226, pred[]{:T(512)S(6)} %compare.42, s32[4,128]{1,0:T(4,128)S(1)} %get-tuple-element.218), kind=kOutput, calls=%fused_computation.22.clone.1 | convolution fusion | flops 201932800 | bytes 542721 | tf_op jit(solution)/shard_map/while/body/eval_jaxpr/gch,qgcl->gqhl/dot_general | solution.py:58
  75.0 1.1 %fusion.66 = f32[8,32,128]{2,1,0:T(8,128)S(1)} fusion(f32[4,128,128]{2,1,0:T(8,128)S(1)} %fusion.65, f32[8,4,128]{2,1,0:T(4,128)S(1)} %dynamic-slice_bitcast_fusion.2, f32[8,32,128]{2,1,0:T(8,128)S(1)} %get-tuple-element.226, pred[]{:T(512)S(6)} %compare.42, s32[4,128]{1,0:T(4,128)S(1)} %get-tuple-element.218), kind=kOutput, calls=%fused_computation.22.clone.1 | convolution fusion | flops 201932800 | bytes 542721 | tf_op jit(solution)/shard_map/while/body/eval_jaxpr/gch,qgcl->gqhl/dot_general | solution.py:58
  76.3 18.5 %while.25 = (s32[]{:T(128)}, f32[24,4,4,128]{3,2,1,0:T(4,128)S(1)}, s32[24,4,128]{2,1,0:T(4,128)S(1)}, f32[4,32,128]{2,1,0:T(8,128)S(1)}, s32[]{:T(128)}) while((s32[]{:T(128)}, f32[24,4,4,128]{3,2,1,0:T(4,128)S(1)}, s32[24,4,128]{2,1,0:T(4,128)S(1)}, f32[4,32,128]{2,1,0:T(8,128)S(1)}, s32[]{:T(128)}) %tuple.75), condition=%wide.region_5.6_spmd, body=%wide.region_3.5_spmd.sunk | while | flops 101342720 | bytes 624717 | solution.py:80
  95.6 3.4 %all-to-all-start.3 = ((f32[4,4,24,128]{3,2,1,0:T(8,128)}), f32[4,4,24,128]{3,2,1,0:T(8,128)S(1)}, u32[]{:S(2)}, u32[]{:S(2)}) async-start(f32[4,4,24,128]{3,2,1,0:T(8,128)} %pad_maximum_fusion.1), calls=%async_computation.3 | async-start | bytes 393216 | tf_op jit(solution)/shard_map/all_to_all | solution.py:130
  99.6 5.6 %all-to-all-done.3 = f32[4,4,24,128]{3,2,1,0:T(8,128)S(1)} async-done(((f32[4,4,24,128]{3,2,1,0:T(8,128)}), f32[4,4,24,128]{3,2,1,0:T(8,128)S(1)}, u32[]{:S(2)}, u32[]{:S(2)}) %all-to-all-start.3) | async-done | bytes 196640 | tf_op jit(solution)/shard_map/all_to_all | solution.py:130
  (211 shorter events, 36.5 us)
Async XLA Ops:
  3.4 7.2 %copy-start = (f32[4,4,8,128]{3,2,1,0:T(8,128)S(1)}, f32[4,4,8,128]{3,2,1,0:T(8,128)}, u32[]{:S(2)}) copy-start(f32[4,4,8,128]{3,2,1,0:T(8,128)} %param.10) | copy-start | bytes 196612
  3.4 12.4 %copy-start.1 = (f32[4,4096]{1,0:T(4,128)S(1)}, f32[4,4096]{1,0:T(4,128)}, u32[]{:S(2)}) copy-start(f32[4,4096]{1,0:T(4,128)} %param.12) | copy-start | bytes 196612
  4.2 21.8 %all-to-all-start.1 = ((f32[4,96,128]{2,0,1:T(4,128)}), f32[4,96,128]{2,0,1:T(4,128)S(1)}, u32[]{:S(2)}, u32[]{:S(2)}) async-start(f32[4,96,128]{2,0,1:T(4,128)} %copy.20), calls=%async_computation.1 | async-start | bytes 393216 | tf_op jit(solution)/shard_map/all_to_all | solution.py:110
  10.6 6.4 %collective-permute-start.1 = (f32[4,1,8,128]{3,2,1,0:T(8,128)S(1)}, f32[4,1,8,128]{3,2,1,0:T(8,128)S(1)}, u32[]{:S(2)}, u32[]{:S(2)}) collective-permute-start(f32[4,1,8,128]{3,2,1,0:T(8,128)S(1)} %get-tuple-element.160), channel_id=1, source_target_pairs={{0,4},{4,8},{8,12},{1,5},{5,9},{9,13},{2,6},{6,10},{10,14},{3,7},{... | collective-permute-start | bytes 49160 | tf_op jit(solution)/shard_map/ppermute | solution.py:15
  14.5 5.6 %collective-permute-start = (f32[4,1,8,128]{3,2,1,0:T(8,128)S(1)}, f32[4,1,8,128]{3,2,1,0:T(8,128)S(1)}, u32[]{:S(2)}, u32[]{:S(2)}) collective-permute-start(f32[4,1,8,128]{3,2,1,0:T(8,128)S(1)} %get-tuple-element.159), channel_id=1, source_target_pairs={{4,0},{8,4},{12,8},{5,1},{9,5},{13,9},{6,2},{10,6},{14,10},{7,3},{... | collective-permute-start | bytes 49160 | tf_op jit(solution)/shard_map/ppermute | solution.py:18
  17.0 12.7 %copy-start.2 = (s32[4096]{0:T(1024)S(1)}, s32[4096]{0:T(1024)}, u32[]{:S(2)}) copy-start(s32[4096]{0:T(1024)} %param.14) | copy-start | bytes 49156
  20.2 10.4 %collective-permute-start.2 = (f32[4,6,1,128]{3,2,1,0:T(1,128)S(1)}, f32[4,6,1,128]{3,2,1,0:T(1,128)S(1)}, u32[]{:S(2)}, u32[]{:S(2)}) collective-permute-start(f32[4,6,1,128]{3,2,1,0:T(1,128)S(1)} %get-tuple-element.158), channel_id=1, source_target_pairs={{2,0},{3,1},{6,4},{7,5},{10,8},{11,9},{14,12},{15,13},{18,16},{19,... | collective-permute-start | bytes 36872 | tf_op jit(solution)/shard_map/ppermute | solution.py:18
  21.5 9.1 %collective-permute-start.3 = (f32[4,6,1,128]{3,2,1,0:T(1,128)S(1)}, f32[4,6,1,128]{3,2,1,0:T(1,128)S(1)}, u32[]{:S(2)}, u32[]{:S(2)}) collective-permute-start(f32[4,6,1,128]{3,2,1,0:T(1,128)S(1)} %get-tuple-element.157), channel_id=1, source_target_pairs={{0,2},{1,3},{4,6},{5,7},{8,10},{9,11},{12,14},{13,15},{16,18},{17,... | collective-permute-start | bytes 36872 | tf_op jit(solution)/shard_map/ppermute | solution.py:15
  26.0 9.9 %all-to-all-start = ((f32[4,96,128]{2,0,1:T(4,128)}), f32[4,96,128]{2,0,1:T(4,128)S(1)}, u32[]{:S(2)}, u32[]{:S(2)}) async-start(f32[4,96,128]{2,0,1:T(4,128)} %copy.19), calls=%async_computation | async-start | bytes 393216 | tf_op jit(solution)/shard_map/all_to_all | solution.py:109
  35.9 8.9 %all-to-all-start.2 = ((s32[1,96,128]{2,0,1:T(1,128)}), s32[1,96,128]{2,0,1:T(1,128)S(1)}, u32[]{:S(2)}, u32[]{:S(2)}) async-start(s32[1,96,128]{2,0,1:T(1,128)} %bitcast.14), calls=%async_computation.2 | async-start | bytes 98304 | tf_op jit(solution)/shard_map/all_to_all | solution.py:111
  44.9 31.3 %copy-start.3 = (f32[4]{0:T(128)S(1)}, f32[4]{0:T(128)}, u32[]{:S(2)}) copy-start(f32[4]{0:T(128)} %param.11) | copy-start | bytes 52
  95.6 9.6 %all-to-all-start.3 = ((f32[4,4,24,128]{3,2,1,0:T(8,128)}), f32[4,4,24,128]{3,2,1,0:T(8,128)S(1)}, u32[]{:S(2)}, u32[]{:S(2)}) async-start(f32[4,4,24,128]{3,2,1,0:T(8,128)} %pad_maximum_fusion.1), calls=%async_computation.3 | async-start | bytes 393216 | tf_op jit(solution)/shard_map/all_to_all | solution.py:130
